TPU v7x, 32 devices: a whole 2x2x4 slice. The times are simulated.
32 devices in a mesh: row: 8 (over y, x, core), col: 4 (over z).
Axes of the slice: x: 2, y: 2, z: 4, core: 2. Of those that a mesh axis runs over, the one named last changes fastest.
Arguments:
- panel_index: int32 [16], replicated, may hold values 0 or 1
- row_sites: int32 [2048], replicated, may hold values from 0 to 2047, each once
- site_coords: float32 [2, 2048], replicated, may hold values from 0 to 1
- new_coords: float32 [2, 2048], P(None, 'col'), may hold values from 0 to 1
- factor_earlier: bfloat16 [2048, 16384], P(None, 'row'), may hold values from -0.0625 to 0.0625
- solved_earlier: bfloat16 [16384, 2048], P('row', 'col'), may hold values from -6 to 6
- panel_inverse: bfloat16 [2048, 2048], P('row'), as said below
- trailing_rhs: float32 [2048, 2048], P('row', 'col'), may hold values from -6 to 6
- factor_trailing: bfloat16 [2048, 2048], P('row'), may hold values from -0.125 to 0.125
- prior_cov: float32 [2048, 2048], P('row', 'col'), may hold values from -4 to 4
Outputs:
- solved_panel: bfloat16 [2048, 2048], P('row', 'col')
- trailing_out: float32 [2048, 2048], P('row', 'col')
- cond_cov: float32 [2048, 2048], P('row', 'col')
Inputs may be any that keep to these rules, and one draw needn't show every extreme that they name: `row_sites`: each site 0 to 2047 appears once. `panel_inverse`: lower triangular, with diagonal entries between 0.5 and 1.5.
All inputs are finite; a program needn't handle non-finite values.
Results may differ from a plain program's by a relative error of at most 0.0049.
Values may be sent and summed in bfloat16 or wider, within the bound.
No kernel may reach another device: no remote copies, remote signals or barrier semaphores. Data moves between devices by JAX's collectives and lax.ppermute only.
A program may use at most 64 MiB of HBM per device.

v0:
```python
import math

import jax
import jax.numpy as jnp
from jax import lax
from jax.sharding import PartitionSpec as P

length_scale = 0.5


def from_root(block, axis, source):
    block = jnp.where(lax.axis_index(axis) == source, block, jnp.zeros_like(block))
    return lax.psum(block, axis)


def matern(distance):
    scaled = distance * (math.sqrt(3.0) / length_scale)
    return (1.0 + scaled) * jnp.exp(-scaled)


def cross_tile(site_coords, chosen_sites, new_coords):
    rows_xy = jnp.take(site_coords, chosen_sites, axis=1)
    delta_x = rows_xy[0][:, None] - new_coords[0][None, :]
    delta_y = rows_xy[1][:, None] - new_coords[1][None, :]
    return matern(jnp.sqrt(delta_x * delta_x + delta_y * delta_y))


def transpose_product(first_rows, second_rows):
    return lax.dot_general(
        first_rows, second_rows, (((0,), (0,)), ((), ())), preferred_element_type=jnp.float32
    )


def per_device(
    panel_index,
    row_sites,
    site_coords,
    new_coords,
    factor_earlier,
    solved_earlier,
    panel_inverse,
    trailing_rhs,
    factor_trailing,
    prior_cov,
):
    row_place = lax.axis_index("row")
    local_rows = panel_inverse.shape[0]
    panel_rows = panel_inverse.shape[1]
    earlier_rows = solved_earlier.shape[0]
    new_cols = new_coords.shape[1]
    class_count = panel_index.shape[0]
    global_rows = row_place * earlier_rows + jnp.arange(earlier_rows, dtype=jnp.int32)
    wanted = jnp.take(panel_index, global_rows % class_count) > 0
    masked = jnp.where(wanted[:, None], solved_earlier, jnp.zeros_like(solved_earlier))
    partial_value = lax.psum_scatter(
        jnp.dot(factor_earlier, masked, preferred_element_type=jnp.float32),
        "row",
        scatter_dimension=0,
        tiled=True,
    )
    own_sites = lax.dynamic_slice_in_dim(row_sites, row_place * local_rows, local_rows, 0)
    cross_cov = cross_tile(site_coords, own_sites, new_coords)
    right_own = (cross_cov - partial_value).astype(jnp.bfloat16)
    solved = jnp.dot(
        panel_inverse,
        lax.all_gather(right_own, "row", axis=0, tiled=True),
        preferred_element_type=jnp.float32,
    ).astype(jnp.bfloat16)
    cov_rows = prior_cov.shape[0]
    source = row_place * cov_rows // new_cols
    offset = row_place * cov_rows - source * new_cols
    gathered = lax.all_gather(solved, "row", axis=0, tiled=True)
    update = jnp.dot(factor_trailing, gathered, preferred_element_type=jnp.float32)
    column_part = lax.dynamic_slice_in_dim(gathered, offset, cov_rows, 1)
    column_block = from_root(column_part, "col", source)
    gram_sum = transpose_product(column_block, gathered)
    trailing_out = trailing_rhs - update
    cond_cov = prior_cov - gram_sum * (1.0 / panel_rows)
    return (solved, trailing_out, cond_cov)


def solution(mesh):
    return jax.shard_map(
        per_device,
        mesh=mesh,
        in_specs=(
            P(),
            P(),
            P(),
            P(None, "col"),
            P(None, "row"),
            P("row", "col"),
            P("row", None),
            P("row", "col"),
            P("row", None),
            P("row", "col"),
        ),
        out_specs=(P("row", "col"), P("row", "col"), P("row", "col")),
        check_vma=False,
    )
```

profile of v0, /device:TPU:2, one launch (start us, length us, event | category | flops | bytes accessed | tf_op | source)
XLA Modules:
  0.0 208.5 jit_solution(7269590678079118435)
XLA Ops:
  7.2 0.1 compare_reduce_fusion
  7.3 0.1 compare_reduce_fusion.2
  7.7 1.9 fusion.14
  9.6 4.4 %compare_select_fusion.3 = s32[2048,1]{0,1:T(1,128)S(1)} fusion(s32[]{:T(128)} %bitcast.12, s32[]{:T(128)} %bitcast.13, s32[]{:T(128)} %bitcast.14, s32[]{:T(128)} %bitcast.15, s32[]{:T(128)} %bitcast.16, s32[]{:T(128)} %bitcast.18, s32[]{:T(128)} %bitcast.17, s32[]{:T(128)S(6)} %mul.38), kind=kLoop, calls=%fused_computation.28 | loop fusion | flops 55296 | bytes 8224 | tf_op jit(solution)/shard_map/jit(_take)/gather | solution.py:53
  14.0 5.7 %fusion.8 = pred[2048]{0:T(1024)(128)(4,1)S(1)} fusion(pred[2048]{0:T(1024)(128)(4,1)S(1)} %get-tuple-element.31, pred[2048]{0:T(1024)(128)(4,1)S(1)} %get-tuple-element.32, pred[2048]{0:T(1024)(128)(4,1)S(1)} %get-tuple-element.33, pred[2048]{0:T(1024)(128)(4,1)S(1)} %get-tuple-element.34, pred[2048]{0:T(1024)(128)(4,1)S(1)} %get-tuple-element.35, ...), kind=kLoop, calls=%fused_computation.42 | loop fusion | flops 59392 | bytes 28712 | tf_op jit(solution)/shard_map/gt | solution.py:53
  19.8 10.5 %convolution_bitcast_fusion = f32[2048,512]{1,0:T(8,128)} fusion(bf16[2048,2048]{1,0:T(8,128)(2,1)} %param.14, bf16[2048,512]{1,0:T(8,128)(2,1)} %param.15, pred[2048]{0:T(1024)(128)(4,1)S(1)} %fusion.8), kind=kOutput, calls=%fused_computation.1 | convolution fusion | flops 4296015872 | bytes 14682112 | tf_op jit(solution)/shard_map/dot_general | solution.py:56
  30.4 0.6 copy-done.3
  31.0 0.4 copy.17
  31.4 0.8 compare_and_fusion
  32.2 0.7 gather_fusion
  32.9 0.1 select_bitcast_fusion
  33.0 0.2 slice_reduce_fusion.1
  33.2 49.6 %reduce-scatter.2.cloned.1.call-done = f32[256,512]{1,0:T(8,128)} async-done(((f32[2048,512]{1,0:T(8,128)}), f32[256,512]{1,0:T(8,128)}) %reduce-scatter.2.cloned.1.call-update) | async-done | bytes 524304 | tf_op jit(solution)/shard_map/reduce_scatter | solution.py:55
  82.8 2.1 %subtract_convert_fusion = bf16[256,512]{1,0:T(8,128)(2,1)} fusion(f32[256,512]{1,0:T(8,128)} %reduce-scatter.2.cloned.1.call-done, f32[512]{0:T(512)S(1)} %bitcast.38, f32[256]{0:T(256)S(1)} %get-tuple-element.10, f32[512]{0:T(512)S(1)} %bitcast.37, f32[256]{0:T(256)S(1)} %get-tuple-element.9), kind=kLoop, calls=%fused_computation.12 | loop fusion | flops 1441792 | bytes 792576 | tf_op jit(solution)/shard_map/convert_element_type | solution.py:63
  85.1 28.0 %all-gather.3.cloned.1.call-done = bf16[2048,512]{1,0:T(8,128)(2,1)} async-done(((bf16[256,512]{1,0:T(8,128)(2,1)}), bf16[2048,512]{1,0:T(8,128)(2,1)}) %all-gather.3.cloned.1.call-update) | async-done | bytes 2097168 | tf_op jit(solution)/shard_map/all_gather | solution.py:66
  113.1 3.0 %fusion.4 = bf16[256,512]{0,1:T(8,128)(2,1)} fusion(bf16[2048,512]{1,0:T(8,128)(2,1)} %all-gather.3.cloned.1.call-done, bf16[256,2048]{1,0:T(8,128)(2,1)S(1)} %copy-done), kind=kOutput, calls=%fused_computation.9 | convolution fusion | flops 537001984 | bytes 3407872 | tf_op jit(solution)/shard_map/dot_general | solution.py:64
  116.3 28.2 %all-gather.5.cloned.1.call-done = bf16[2048,512]{0,1:T(8,128)(2,1)} async-done(((bf16[256,512]{0,1:T(8,128)(2,1)}), bf16[2048,512]{0,1:T(8,128)(2,1)}) %all-gather.5.cloned.1.call-update) | async-done | bytes 2097168 | tf_op jit(solution)/shard_map/all_gather | solution.py:72
  144.4 2.6 %dynamic-slice_select_fusion = bf16[2048,256]{0,1:T(8,128)(2,1)} fusion(bf16[2048,512]{0,1:T(8,128)(2,1)} %all-gather.5.cloned.1.call-done, s32[]{:T(128)S(6)} %select_n.90, pred[]{:T(512)S(6)} %eq.5), kind=kLoop, calls=%fused_computation.10 | loop fusion | flops 524288 | bytes 2097157 | tf_op jit(solution)/shard_map/jit(_where)/select_n | solution.py:12
  147.0 2.0 copy.18
  149.1 0.8 copy.19
  149.9 2.9 %fusion.3 = f32[256,512]{0,1:T(8,128)} fusion(f32[256,512]{0,1:T(8,128)} %copy.18, bf16[2048,512]{0,1:T(8,128)(2,1)S(1)} %copy-done.1, bf16[256,2048]{1,0:T(8,128)(2,1)} %param.18), kind=kOutput, calls=%fused_computation.7 | convolution fusion | flops 537001984 | bytes 4194304 | tf_op jit(solution)/shard_map/dot_general | solution.py:73
  152.8 2.0 copy.20
  154.9 44.2 %all-reduce.2.cloned.1.call-done = bf16[2048,256]{0,1:T(8,128)(2,1)} async-done(((bf16[2048,256]{0,1:T(8,128)(2,1)}), bf16[2048,256]{0,1:T(8,128)(2,1)}) %all-reduce.2.cloned.1.call-update) | async-done | bytes 1048592 | tf_op jit(solution)/shard_map/psum | solution.py:13
  199.1 2.9 %fusion.2 = f32[256,512]{1,0:T(8,128)} fusion(f32[256,512]{1,0:T(8,128)} %param.19, bf16[2048,256]{0,1:T(8,128)(2,1)} %all-reduce.2.cloned.1.call-done, bf16[2048,512]{0,1:T(8,128)(2,1)S(1)} %copy-done.1), kind=kOutput, calls=%fused_computation.5 | convolution fusion | flops 537133056 | bytes 4194304 | tf_op jit(solution)/shard_map/dot_general | solution.py:29
  (22 shorter events, 0.5 us)
Async XLA Ops:
  7.2 105.9 %copy-start = (bf16[256,2048]{1,0:T(8,128)(2,1)S(1)}, bf16[256,2048]{1,0:T(8,128)(2,1)}, u32[]{:S(2)}) copy-start(bf16[256,2048]{1,0:T(8,128)(2,1)} %param.16) | copy-start | bytes 3145732
  7.2 75.7 %reduce-scatter.2.cloned.1.call-start = ((), (), s32[]{:S(2)}) async-start(), calls=%async_computation.1 | async-start | bytes 4718592 | tf_op jit(solution)/shard_map/reduce_scatter | solution.py:55
  30.3 0.7 copy-start.3
  30.3 2.9 %copy-start.4 = (f32[2,512]{1,0:T(2,128)S(1)}, f32[2,512]{1,0:T(2,128)}, u32[]{:S(2)}) copy-start(f32[2,512]{1,0:T(2,128)} %param.13) | copy-start | bytes 12292
  30.3 82.8 %all-gather.3.cloned.1.call-start = ((), (), s32[]{:S(2)}) async-start(), calls=%async_computation.2 | async-start | bytes 2359296 | tf_op jit(solution)/shard_map/all_gather | solution.py:66
  85.0 59.4 %all-gather.5.cloned.1.call-start = ((), (), s32[]{:S(2)}) async-start(), calls=%async_computation.3 | async-start | bytes 2359296 | tf_op jit(solution)/shard_map/all_gather | solution.py:72
  116.2 82.9 %all-reduce.2.cloned.1.call-start = ((), (), s32[]{:S(2)}) async-start(), calls=%async_computation.4 | async-start | bytes 2097152 | tf_op jit(solution)/shard_map/psum | solution.py:13
  116.2 32.8 %copy-start.2 = (bf16[256,512]{0,1:T(8,128)(2,1)S(1)}, bf16[256,512]{0,1:T(8,128)(2,1)}, u32[]{:S(2)}) copy-start(bf16[256,512]{0,1:T(8,128)(2,1)} %fusion.4) | copy-start | bytes 786436
  144.4 5.5 %copy-start.1 = (bf16[2048,512]{0,1:T(8,128)(2,1)S(1)}, bf16[2048,512]{0,1:T(8,128)(2,1)}, u32[]{:S(2)}) copy-start(bf16[2048,512]{0,1:T(8,128)(2,1)} %all-gather.5.cloned.1.call-done) | copy-start | bytes 6291460
Sparse Core Ops, SparseCore 0:
  30.4 52.3 reduce-scatter.1
  85.3 27.7 all-gather.2
  116.3 28.0 all-gather.4
  147.1 51.8 all-reduce.1
where the time goes:
time: 211 us; the launch traced here: 209 us
  waiting for transfers between devices  150 us (71%)
  matrix products  19.3 us (9%)
  other arithmetic  16.2 us (8%)
  between operations  13.9 us (7%)
  local copies, waits for them, and re-layouts  8.83 us (4%)
    reduce_scatter x1, waiting for transfers between devices, per_device(): lax.psum_scatter(jnp.dot(factor_earlier, masked, preferred_element_type=j...  49.6 us
    psum x1, waiting for transfers between devices, from_root(): return lax.psum(block, axis)  44.2 us
    all_gather x1, waiting for transfers between devices, per_device(): gathered = lax.all_gather(solved, 'row', axis=0, tiled=True)  28.2 us
    all_gather x1, waiting for transfers between devices, per_device(): lax.all_gather(right_own, 'row', axis=0, tiled=True)  28 us
    dot_general x1, matrix products, per_device(): jnp.dot(factor_earlier, masked, preferred_element_type=jnp.float32)  10.5 us
    unnamed x14, local copies, waits for them, and re-layouts  5.95 us
    gt x1, other arithmetic, per_device(): wanted = jnp.take(panel_index, global_rows % class_count) > 0  5.73 us
    gather x6, other arithmetic, per_device(): wanted = jnp.take(panel_index, global_rows % class_count) > 0  4.84 us
  transfers between devices with their start and end apart: 4, of which 4 were waited for; matrix products, arithmetic and copies ran while one was open for 5% of the time, Pallas kernels for 0%

commit v1 on v0

v1 whole, which is shorter than its diff:
```python
import math

import jax
import jax.numpy as jnp
from jax import lax
from jax.sharding import PartitionSpec as P

length_scale = 0.5
CORES = 2


def matern(distance):
    scaled = distance * (math.sqrt(3.0) / length_scale)
    return (1.0 + scaled) * jnp.exp(-scaled)


def cross_tile(site_coords, chosen_sites, new_coords):
    rows_xy = jnp.take(site_coords, chosen_sites, axis=1)
    delta_x = rows_xy[0][:, None] - new_coords[0][None, :]
    delta_y = rows_xy[1][:, None] - new_coords[1][None, :]
    return matern(jnp.sqrt(delta_x * delta_x + delta_y * delta_y))


def product(first, second):
    return jnp.dot(first, second, preferred_element_type=jnp.float32)


def transpose_product(first_rows, second_rows):
    return lax.dot_general(
        first_rows, second_rows, (((0,), (0,)), ((), ())), preferred_element_type=jnp.float32
    )


def make_per_device(row_count, col_count):
    chips = row_count // CORES

    def to_partner(value):
        return lax.ppermute(value, "row", [(r, r ^ 1) for r in range(row_count)])

    def to_chip(value, step):
        return lax.ppermute(value, "row", [(r, r ^ (CORES * step)) for r in range(row_count)])

    def around_col(value, hop):
        pairs = []
        for r in range(row_count):
            root = r // CORES
            begin = (root + hop - 1) % col_count
            end = (root + hop) % col_count
            pairs.append((r * col_count + begin, r * col_count + end))
        return lax.ppermute(value, ("row", "col"), pairs)

    def per_device(
        panel_index,
        row_sites,
        site_coords,
        new_coords,
        factor_earlier,
        solved_earlier,
        panel_inverse,
        trailing_rhs,
        factor_trailing,
        prior_cov,
    ):
        row_place = lax.axis_index("row")
        col_place = lax.axis_index("col")
        core = row_place % CORES
        chip = row_place // CORES
        local_rows = panel_inverse.shape[0]
        panel_rows = panel_inverse.shape[1]
        earlier_rows = solved_earlier.shape[0]
        new_cols = new_coords.shape[1]
        cov_rows = prior_cov.shape[0]
        class_count = panel_index.shape[0]
        half = new_cols // CORES
        chip_rows = local_rows * CORES

        if earlier_rows % class_count == 0:
            flags = jnp.tile(panel_index, earlier_rows // class_count)
        else:
            global_rows = row_place * earlier_rows + jnp.arange(earlier_rows, dtype=jnp.int32)
            flags = jnp.take(panel_index, global_rows % class_count)
        flags = flags.astype(jnp.bfloat16)[:, None]
        other_cols = lax.dynamic_slice_in_dim(solved_earlier, (1 - core) * half, half, 1) * flags
        own_cols = lax.dynamic_slice_in_dim(solved_earlier, core * half, half, 1) * flags

        inverse_other = to_partner(panel_inverse)
        partial_other = product(factor_earlier, other_cols).astype(jnp.bfloat16)
        partial_got = to_partner(partial_other)
        partial_own = product(factor_earlier, own_cols)
        chip_sum = partial_own + partial_got.astype(jnp.float32)

        def chunk(step):
            return lax.dynamic_slice_in_dim(chip_sum, (chip ^ step) * chip_rows, chip_rows, 0)

        arrived = [to_chip(chunk(step).astype(jnp.bfloat16), step) for step in range(1, chips)]

        def relative(value):
            return jnp.concatenate(
                [
                    lax.dynamic_slice_in_dim(value, (chip ^ step) * chip_rows, chip_rows, 1)
                    for step in range(chips)
                ],
                axis=1,
            )

        first_rows = jnp.where(core == 0, panel_inverse, inverse_other)
        second_rows = jnp.where(core == 0, inverse_other, panel_inverse)
        inverse_chip = relative(jnp.concatenate([first_rows, second_rows], axis=0))
        trailing_factor = relative(factor_trailing)

        own_sites = lax.dynamic_slice_in_dim(row_sites, chip * chip_rows, chip_rows, 0)
        half_coords = lax.dynamic_slice_in_dim(new_coords, core * half, half, 1)
        cross_cov = cross_tile(site_coords, own_sites, half_coords)

        total = chunk(0)
        for piece in arrived:
            total = total + piece.astype(jnp.float32)
        right_own = (cross_cov - total).astype(jnp.bfloat16)
        right_parts = [right_own] + [to_chip(right_own, step) for step in range(1, chips)]
        solved_own = product(inverse_chip, jnp.concatenate(right_parts, axis=0)).astype(
            jnp.bfloat16
        )

        away = lax.dynamic_slice_in_dim(solved_own, (1 - core) * local_rows, local_rows, 0)
        home = lax.dynamic_slice_in_dim(solved_own, core * local_rows, local_rows, 0)
        back = to_partner(away)

        def both(mine, theirs):
            return jnp.concatenate(
                [jnp.where(core == 0, mine, theirs), jnp.where(core == 0, theirs, mine)], axis=1
            )

        solved = both(home, back)

        solved_parts = [solved_own] + [to_chip(solved_own, step) for step in range(1, chips)]
        mine = jnp.concatenate(solved_parts, axis=0)
        theirs = to_partner(mine)
        gathered = both(mine, theirs)
        trailing_out = trailing_rhs - product(trailing_factor, gathered)

        if new_cols == CORES * cov_rows and chips == col_count:
            hops_away = (col_place - chip) % col_count
            blocks = []
            for part in solved_parts:
                moving = part
                block = part
                for hop in range(1, col_count):
                    moving = around_col(moving, hop)
                    block = jnp.where(hops_away == hop, moving, block)
                blocks.append(block)
            column_block = jnp.concatenate(blocks, axis=0)
        else:
            source = row_place * cov_rows // new_cols
            offset = row_place * cov_rows - source * new_cols
            column_block = lax.dynamic_slice_in_dim(gathered, offset, cov_rows, 1)
            column_block = jnp.where(col_place == source, column_block, jnp.zeros_like(column_block))
            column_block = lax.psum(column_block, "col")
        cond_cov = prior_cov - transpose_product(column_block, gathered) * (1.0 / panel_rows)
        return (solved, trailing_out, cond_cov)

    return per_device


def solution(mesh):
    return jax.shard_map(
        make_per_device(mesh.shape["row"], mesh.shape["col"]),
        mesh=mesh,
        in_specs=(
            P(),
            P(),
            P(),
            P(None, "col"),
            P(None, "row"),
            P("row", "col"),
            P("row", None),
            P("row", "col"),
            P("row", None),
            P("row", "col"),
        ),
        out_specs=(P("row", "col"), P("row", "col"), P("row", "col")),
        check_vma=False,
    )
```

time: 211 us -> 103 us (0.49)
  waiting for transfers between devices: 150 us -> 49.6 us
  starting transfers between devices: 0.16 us -> 24.7 us
  between operations: 13.9 us -> 1.08 us
  other arithmetic: 16.2 us -> 6.1 us
  local copies, waits for them, and re-layouts: 8.83 us -> 2.79 us
    all_gather x2 -> x0, waiting for transfers between devices: 56.2 us -> none  [the longest x1 28.2 us: per_device(): gathered = lax.all_gather(solved, 'row', axis=0, tiled=True)]
    reduce_scatter x1 -> x0, waiting for transfers between devices: 49.6 us -> none  [per_device(): lax.psum_scatter(jnp.dot(factor_earlier, masked, preferred_element_type=j...]
    ppermute x0 -> x25, waiting for transfers between devices: none -> 49.6 us  [the longest x9 25.7 us: to_chip(): lax.ppermute(value, 'row', [(r, r ^ CORES * step) for r in range(row_coun...]
    psum x1 -> x0, waiting for transfers between devices: 44.2 us -> none  [from_root(): return lax.psum(block, axis)]
    ppermute x0 -> x25, starting transfers between devices: none -> 24.7 us  [the longest x9 13.5 us: to_chip(): lax.ppermute(value, 'row', [(r, r ^ CORES * step) for r in range(row_coun...]
    gt x1 -> x0, other arithmetic: 5.73 us -> none  [per_device(): wanted = jnp.take(panel_index, global_rows % class_count) > 0]
    unnamed x14 -> x15, local copies, waits for them, and re-layouts: 5.95 us -> 1.01 us
    gather x6 -> x0, other arithmetic: 4.84 us -> none  [per_device(): wanted = jnp.take(panel_index, global_rows % class_count) > 0]
  transfers between devices with their start and end apart: 4 -> 25, of which waited for: 4 -> 12; matrix products, arithmetic and copies ran while one was open for 5% -> 13% of each run, Pallas kernels for 0% -> 0%
where the time goes in v1:
time: 103 us; the launch traced here: 102 us
  waiting for transfers between devices  49.6 us (48%)
  starting transfers between devices  24.7 us (24%)
  matrix products  18 us (17%)
  other arithmetic  6.1 us (6%)
  local copies, waits for them, and re-layouts  2.79 us (3%)
  between operations  1.08 us (1%)
    ppermute x9, waiting for transfers between devices, to_chip(): lax.ppermute(value, 'row', [(r, r ^ CORES * step) for r in range(row_coun...  25.7 us
    ppermute x12, waiting for transfers between devices, around_col(): return lax.ppermute(value, ('row', 'col'), pairs)  23.6 us
    dot_general x4, matrix products, product(): return jnp.dot(first, second, preferred_element_type=jnp.float32)  16.4 us
    ppermute x9, starting transfers between devices, to_chip(): lax.ppermute(value, 'row', [(r, r ^ CORES * step) for r in range(row_coun...  13.5 us
    ppermute x12, starting transfers between devices, around_col(): return lax.ppermute(value, ('row', 'col'), pairs)  10.5 us
  transfers between devices with their start and end apart: 25, of which 12 were waited for; matrix products, arithmetic and copies ran while one was open for 13% of the time, Pallas kernels for 0%

profile of v1, /device:TPU:2, one launch (start us, length us, event | category | flops | bytes accessed | tf_op | source)
XLA Modules:
  0.0 102.2 jit_solution(15057364345198062670)
XLA Ops:
  1.4 7.5 %fusion = bf16[2048,256]{0,1:T(8,128)(2,1)} fusion(bf16[2048,2048]{1,0:T(8,128)(2,1)} %param.14, bf16[2048,512]{1,0:T(8,128)(2,1)} %param.15, s32[]{:T(128)S(6)} %select_n.159, bf16[2048]{0:T(1024)(128)(2,1)S(1)} %convert_element_type.45), kind=kOutput, calls=%fused_computation.11 | convolution fusion | flops 2150105088 | bytes 10489860 | tf_op jit(solution)/shard_map/dot_general | solution.py:25
  12.0 6.7 %convert_add_fusion = f32[2048,256]{0,1:T(8,128)S(1)} fusion(bf16[2048,256]{0,1:T(8,128)(2,1)} %collective-permute-done.1, bf16[2048,2048]{1,0:T(8,128)(2,1)} %param.14, bf16[2048,512]{1,0:T(8,128)(2,1)} %param.15, s32[]{:T(128)S(6)} %select_n.158, bf16[2048]{0:T(1024)(128)(2,1)S(1)} %convert_element_type.45), kind=kOutput, calls=%fused_computation.21 | convolution fusion | flops 2150629376 | bytes 12587012 | tf_op jit(solution)/shard_map/dot_general | solution.py:25
  18.9 2.0 %collective-permute-start.3 = (bf16[512,256]{0,1:T(8,128)(2,1)S(1)}, bf16[512,256]{0,1:T(8,128)(2,1)}, u32[]{:S(2)}, u32[]{:S(2)}) collective-permute-start(bf16[512,256]{0,1:T(8,128)(2,1)S(1)} %get-tuple-element.11), channel_id=1, source_target_pairs={{0,16},{4,20},{8,24},{12,28},{16,0},{20,4},{24,8},{28,12},{1,17},{... | collective-permute-start | bytes 786440 | tf_op jit(solution)/shard_map/ppermute | solution.py:41
  20.9 1.4 %collective-permute-start.4 = (bf16[512,256]{0,1:T(8,128)(2,1)S(1)}, bf16[512,256]{0,1:T(8,128)(2,1)}, u32[]{:S(2)}, u32[]{:S(2)}) collective-permute-start(bf16[512,256]{0,1:T(8,128)(2,1)S(1)} %get-tuple-element.10), channel_id=1, source_target_pairs={{0,24},{4,28},{8,16},{12,20},{16,8},{20,12},{24,0},{28,4},{1,25},{... | collective-permute-start | bytes 786440 | tf_op jit(solution)/shard_map/ppermute | solution.py:41
  22.9 5.2 %collective-permute-done.2 = bf16[512,256]{0,1:T(8,128)(2,1)} collective-permute-done((bf16[512,256]{0,1:T(8,128)(2,1)S(1)}, bf16[512,256]{0,1:T(8,128)(2,1)}, u32[]{:S(2)}, u32[]{:S(2)}) %collective-permute-start.2) | collective-permute-done | bytes 262176 | tf_op jit(solution)/shard_map/ppermute | solution.py:41
  28.1 4.0 %collective-permute-done.3 = bf16[512,256]{0,1:T(8,128)(2,1)} collective-permute-done((bf16[512,256]{0,1:T(8,128)(2,1)S(1)}, bf16[512,256]{0,1:T(8,128)(2,1)}, u32[]{:S(2)}, u32[]{:S(2)}) %collective-permute-start.3) | collective-permute-done | bytes 262176 | tf_op jit(solution)/shard_map/ppermute | solution.py:41
  32.1 1.7 %collective-permute-done.4 = bf16[512,256]{0,1:T(8,128)(2,1)} collective-permute-done((bf16[512,256]{0,1:T(8,128)(2,1)S(1)}, bf16[512,256]{0,1:T(8,128)(2,1)}, u32[]{:S(2)}, u32[]{:S(2)}) %collective-permute-start.4) | collective-permute-done | bytes 262176 | tf_op jit(solution)/shard_map/ppermute | solution.py:41
  33.9 1.8 %subtract_convert_fusion = bf16[512,256]{0,1:T(8,128)(2,1)S(1)} fusion(bf16[512,256]{0,1:T(8,128)(2,1)} %collective-permute-done.4, bf16[512,256]{0,1:T(8,128)(2,1)} %collective-permute-done.3, bf16[512,256]{0,1:T(8,128)(2,1)} %collective-permute-done.2, f32[2048,256]{0,1:T(8,128)} %copy-done.2, s32[]{:T(128)S(6)} %select_n.152, f32[256]{0:T(256)S(1)} %bitcast.13, ...), kind=kLoop, calls=%fused_computation.62 | loop fusion | flops 2228224 | bytes 1579012 | tf_op jit(solution)/shard_map/convert_element_type | solution.py:118
  36.5 1.5 %collective-permute-start.6 = (bf16[512,256]{0,1:T(8,128)(2,1)S(1)}, bf16[512,256]{0,1:T(8,128)(2,1)S(1)}, u32[]{:S(2)}, u32[]{:S(2)}) collective-permute-start(bf16[512,256]{0,1:T(8,128)(2,1)S(1)} %subtract_convert_fusion), channel_id=1, source_target_pairs={{0,16},{4,20},{8,24},{12,28},{16,0},{20,4},{24,8},{28,12},{1,17},{... | collective-permute-start | bytes 786440 | tf_op jit(solution)/shard_map/ppermute | solution.py:41
  39.6 5.3 %collective-permute-done.5 = bf16[512,256]{0,1:T(8,128)(2,1)S(1)} collective-permute-done((bf16[512,256]{0,1:T(8,128)(2,1)S(1)}, bf16[512,256]{0,1:T(8,128)(2,1)S(1)}, u32[]{:S(2)}, u32[]{:S(2)}) %collective-permute-start.5) | collective-permute-done | bytes 262176 | tf_op jit(solution)/shard_map/ppermute | solution.py:41
  44.9 4.2 %collective-permute-done.6 = bf16[512,256]{0,1:T(8,128)(2,1)S(1)} collective-permute-done((bf16[512,256]{0,1:T(8,128)(2,1)S(1)}, bf16[512,256]{0,1:T(8,128)(2,1)S(1)}, u32[]{:S(2)}, u32[]{:S(2)}) %collective-permute-start.6) | collective-permute-done | bytes 262176 | tf_op jit(solution)/shard_map/ppermute | solution.py:41
  49.8 1.5 %collective-permute-start.9 = (bf16[512,256]{1,0:T(8,128)(2,1)S(1)}, bf16[512,256]{1,0:T(8,128)(2,1)S(1)}, u32[]{:S(2)}, u32[]{:S(2)}) collective-permute-start(bf16[512,256]{1,0:T(8,128)(2,1)S(1)} %fusion.14), channel_id=1, source_target_pairs={{0,8},{4,12},{8,0},{12,4},{16,24},{20,28},{24,16},{28,20},{1,9},{5... | collective-permute-start | bytes 786440 | tf_op jit(solution)/shard_map/ppermute | solution.py:41
  53.3 3.7 %collective-permute-start.11 = (bf16[512,256]{1,0:T(8,128)(2,1)S(1)}, bf16[512,256]{1,0:T(8,128)(2,1)S(1)}, u32[]{:S(2)}, u32[]{:S(2)}) collective-permute-start(bf16[512,256]{1,0:T(8,128)(2,1)S(1)} %fusion.14), channel_id=1, source_target_pairs={{0,24},{4,28},{8,16},{12,20},{16,8},{20,12},{24,0},{28,4},{1,25},{... | collective-permute-start | bytes 786440 | tf_op jit(solution)/shard_map/ppermute | solution.py:41
  57.0 1.9 %collective-permute-done.9 = bf16[512,256]{1,0:T(8,128)(2,1)S(1)} collective-permute-done((bf16[512,256]{1,0:T(8,128)(2,1)S(1)}, bf16[512,256]{1,0:T(8,128)(2,1)S(1)}, u32[]{:S(2)}, u32[]{:S(2)}) %collective-permute-start.9) | collective-permute-done | bytes 262176 | tf_op jit(solution)/shard_map/ppermute | solution.py:41
  60.3 3.4 %collective-permute-done.10 = bf16[512,256]{1,0:T(8,128)(2,1)S(1)} collective-permute-done((bf16[512,256]{1,0:T(8,128)(2,1)S(1)}, bf16[512,256]{1,0:T(8,128)(2,1)S(1)}, u32[]{:S(2)}, u32[]{:S(2)}) %collective-permute-start.10) | collective-permute-done | bytes 262176 | tf_op jit(solution)/shard_map/ppermute | solution.py:41
  66.9 1.3 %collective-permute-start.15 = (bf16[512,256]{1,0:T(8,128)(2,1)S(1)}, bf16[512,256]{1,0:T(8,128)(2,1)S(1)}, u32[]{:S(2)}, u32[]{:S(2)}) collective-permute-start(bf16[512,256]{1,0:T(8,128)(2,1)S(1)} %collective-permute-done.14), channel_id=1, source_target_pairs={{2,3},{6,7},{11,8},{15,12},{16,17},{20,21},{25,26},{29,30}} | collective-permute-start | bytes 786440 | tf_op jit(solution)/shard_map/ppermute | solution.py:50
  69.7 1.3 %collective-permute-start.18 = (bf16[512,256]{1,0:T(8,128)(2,1)S(1)}, bf16[512,256]{1,0:T(8,128)(2,1)S(1)}, u32[]{:S(2)}, u32[]{:S(2)}) collective-permute-start(bf16[512,256]{1,0:T(8,128)(2,1)S(1)} %collective-permute-done.17), channel_id=1, source_target_pairs={{2,3},{6,7},{11,8},{15,12},{16,17},{20,21},{25,26},{29,30}} | collective-permute-start | bytes 786440 | tf_op jit(solution)/shard_map/ppermute | solution.py:50
  73.1 1.3 %collective-permute-start.24 = (bf16[512,256]{1,0:T(8,128)(2,1)S(1)}, bf16[512,256]{1,0:T(8,128)(2,1)S(1)}, u32[]{:S(2)}, u32[]{:S(2)}) collective-permute-start(bf16[512,256]{1,0:T(8,128)(2,1)S(1)} %collective-permute-done.23), channel_id=1, source_target_pairs={{2,3},{6,7},{11,8},{15,12},{16,17},{20,21},{25,26},{29,30}} | collective-permute-start | bytes 786440 | tf_op jit(solution)/shard_map/ppermute | solution.py:50
  74.4 6.9 %collective-permute-done.15 = bf16[512,256]{1,0:T(8,128)(2,1)S(1)} collective-permute-done((bf16[512,256]{1,0:T(8,128)(2,1)S(1)}, bf16[512,256]{1,0:T(8,128)(2,1)S(1)}, u32[]{:S(2)}, u32[]{:S(2)}) %collective-permute-start.15) | collective-permute-done | bytes 262176 | tf_op jit(solution)/shard_map/ppermute | solution.py:50
  81.3 6.8 %collective-permute-done.18 = bf16[512,256]{1,0:T(8,128)(2,1)S(1)} collective-permute-done((bf16[512,256]{1,0:T(8,128)(2,1)S(1)}, bf16[512,256]{1,0:T(8,128)(2,1)S(1)}, u32[]{:S(2)}, u32[]{:S(2)}) %collective-permute-start.18) | collective-permute-done | bytes 262176 | tf_op jit(solution)/shard_map/ppermute | solution.py:50
  88.2 5.2 %collective-permute-done.21 = bf16[512,256]{1,0:T(8,128)(2,1)S(1)} collective-permute-done((bf16[512,256]{1,0:T(8,128)(2,1)S(1)}, bf16[512,256]{1,0:T(8,128)(2,1)S(1)}, u32[]{:S(2)}, u32[]{:S(2)}) %collective-permute-start.21) | collective-permute-done | bytes 262176 | tf_op jit(solution)/shard_map/ppermute | solution.py:50
  93.5 4.7 %collective-permute-done.24 = bf16[512,256]{1,0:T(8,128)(2,1)S(1)} collective-permute-done((bf16[512,256]{1,0:T(8,128)(2,1)S(1)}, bf16[512,256]{1,0:T(8,128)(2,1)S(1)}, u32[]{:S(2)}, u32[]{:S(2)}) %collective-permute-start.24) | collective-permute-done | bytes 262176 | tf_op jit(solution)/shard_map/ppermute | solution.py:50
  99.2 1.5 %fusion.13 = f32[256,512]{1,0:T(8,128)} fusion(f32[256,512]{1,0:T(8,128)S(1)} %copy-done.5, bf16[2048,256]{1,0:T(8,128)(2,1)S(1)} %get-tuple-element.8, bf16[2048,256]{1,0:T(8,128)(2,1)S(1)} %get-tuple-element.7, bf16[512,256]{1,0:T(8,128)(2,1)S(1)} %select_select_fusion, bf16[512,256]{1,0:T(8,128)(2,1)S(1)} %select_select_fusion.1, ...), kind=kOutput, calls=%fused_computation.26 | convolution fusion | flops 545521664 | bytes 4194304 | tf_op jit(solution)/shard_map/dot_general | solution.py:29
  100.7 1.5 %fusion.11 = f32[256,512]{1,0:T(8,128)} fusion(f32[256,512]{1,0:T(8,128)S(1)} %copy-done.6, bf16[2048,256]{1,0:T(8,128)(2,1)S(1)} %get-tuple-element.8, bf16[2048,256]{1,0:T(8,128)(2,1)S(1)} %get-tuple-element.7, bf16[256,512]{1,0:T(8,128)(2,1)S(1)} %get-tuple-element.20, bf16[256,512]{1,0:T(8,128)(2,1)S(1)} %get-tuple-element.21, ...), kind=kOutput, calls=%fused_computation.24 | convolution fusion | flops 545390592 | bytes 4194304 | tf_op jit(solution)/shard_map/dot_general | solution.py:25
  (69 shorter events, 18.8 us)
Async XLA Ops:
  9.0 30.2 %collective-permute-start = (bf16[256,2048]{1,0:T(8,128)(2,1)S(1)}, bf16[256,2048]{1,0:T(8,128)(2,1)S(1)}, u32[]{:S(2)}, u32[]{:S(2)}) collective-permute-start(bf16[256,2048]{1,0:T(8,128)(2,1)S(1)} %copy-done), channel_id=1, source_target_pairs={{0,4},{4,0},{8,12},{12,8},{16,20},{20,16},{24,28},{28,24},{1,5},{5... | collective-permute-start | bytes 3145736 | tf_op jit(solution)/shard_map/ppermute | solution.py:38
  18.8 9.3 %collective-permute-start.2 = (bf16[512,256]{0,1:T(8,128)(2,1)S(1)}, bf16[512,256]{0,1:T(8,128)(2,1)}, u32[]{:S(2)}, u32[]{:S(2)}) collective-permute-start(bf16[512,256]{0,1:T(8,128)(2,1)S(1)} %get-tuple-element.9), channel_id=1, source_target_pairs={{0,8},{4,12},{8,0},{12,4},{16,24},{20,28},{24,16},{28,20},{1,9},{5... | collective-permute-start | bytes 786440 | tf_op jit(solution)/shard_map/ppermute | solution.py:41
  18.9 13.3 %collective-permute-start.3 = (bf16[512,256]{0,1:T(8,128)(2,1)S(1)}, bf16[512,256]{0,1:T(8,128)(2,1)}, u32[]{:S(2)}, u32[]{:S(2)}) collective-permute-start(bf16[512,256]{0,1:T(8,128)(2,1)S(1)} %get-tuple-element.11), channel_id=1, source_target_pairs={{0,16},{4,20},{8,24},{12,28},{16,0},{20,4},{24,8},{28,12},{1,17},{... | collective-permute-start | bytes 786440 | tf_op jit(solution)/shard_map/ppermute | solution.py:41
  20.9 13.0 %collective-permute-start.4 = (bf16[512,256]{0,1:T(8,128)(2,1)S(1)}, bf16[512,256]{0,1:T(8,128)(2,1)}, u32[]{:S(2)}, u32[]{:S(2)}) collective-permute-start(bf16[512,256]{0,1:T(8,128)(2,1)S(1)} %get-tuple-element.10), channel_id=1, source_target_pairs={{0,24},{4,28},{8,16},{12,20},{16,8},{20,12},{24,0},{28,4},{1,25},{... | collective-permute-start | bytes 786440 | tf_op jit(solution)/shard_map/ppermute | solution.py:41
  35.6 9.2 %collective-permute-start.5 = (bf16[512,256]{0,1:T(8,128)(2,1)S(1)}, bf16[512,256]{0,1:T(8,128)(2,1)S(1)}, u32[]{:S(2)}, u32[]{:S(2)}) collective-permute-start(bf16[512,256]{0,1:T(8,128)(2,1)S(1)} %subtract_convert_fusion), channel_id=1, source_target_pairs={{0,8},{4,12},{8,0},{12,4},{16,24},{20,28},{24,16},{28,20},{1,9},{5... | collective-permute-start | bytes 786440 | tf_op jit(solution)/shard_map/ppermute | solution.py:41
  36.5 12.6 %collective-permute-start.6 = (bf16[512,256]{0,1:T(8,128)(2,1)S(1)}, bf16[512,256]{0,1:T(8,128)(2,1)S(1)}, u32[]{:S(2)}, u32[]{:S(2)}) collective-permute-start(bf16[512,256]{0,1:T(8,128)(2,1)S(1)} %subtract_convert_fusion), channel_id=1, source_target_pairs={{0,16},{4,20},{8,24},{12,28},{16,0},{20,4},{24,8},{28,12},{1,17},{... | collective-permute-start | bytes 786440 | tf_op jit(solution)/shard_map/ppermute | solution.py:41
  38.0 11.1 %collective-permute-start.7 = (bf16[512,256]{0,1:T(8,128)(2,1)S(1)}, bf16[512,256]{0,1:T(8,128)(2,1)S(1)}, u32[]{:S(2)}, u32[]{:S(2)}) collective-permute-start(bf16[512,256]{0,1:T(8,128)(2,1)S(1)} %subtract_convert_fusion), channel_id=1, source_target_pairs={{0,24},{4,28},{8,16},{12,20},{16,8},{20,12},{24,0},{28,4},{1,25},{... | collective-permute-start | bytes 786440 | tf_op jit(solution)/shard_map/ppermute | solution.py:41
  49.8 9.0 %collective-permute-start.9 = (bf16[512,256]{1,0:T(8,128)(2,1)S(1)}, bf16[512,256]{1,0:T(8,128)(2,1)S(1)}, u32[]{:S(2)}, u32[]{:S(2)}) collective-permute-start(bf16[512,256]{1,0:T(8,128)(2,1)S(1)} %fusion.14), channel_id=1, source_target_pairs={{0,8},{4,12},{8,0},{12,4},{16,24},{20,28},{24,16},{28,20},{1,9},{5... | collective-permute-start | bytes 786440 | tf_op jit(solution)/shard_map/ppermute | solution.py:41
  51.4 8.2 %collective-permute-start.13 = (bf16[512,256]{1,0:T(8,128)(2,1)S(1)}, bf16[512,256]{1,0:T(8,128)(2,1)S(1)}, u32[]{:S(2)}, u32[]{:S(2)}) collective-permute-start(bf16[512,256]{1,0:T(8,128)(2,1)S(1)} %fusion.14), channel_id=1, source_target_pairs={{0,1},{4,5},{9,10},{13,14},{18,19},{22,23},{27,24},{31,28}} | collective-permute-start | bytes 786440 | tf_op jit(solution)/shard_map/ppermute | solution.py:50
  52.0 11.6 %collective-permute-start.10 = (bf16[512,256]{1,0:T(8,128)(2,1)S(1)}, bf16[512,256]{1,0:T(8,128)(2,1)S(1)}, u32[]{:S(2)}, u32[]{:S(2)}) collective-permute-start(bf16[512,256]{1,0:T(8,128)(2,1)S(1)} %fusion.14), channel_id=1, source_target_pairs={{0,16},{4,20},{8,24},{12,28},{16,0},{20,4},{24,8},{28,12},{1,17},{... | collective-permute-start | bytes 786440 | tf_op jit(solution)/shard_map/ppermute | solution.py:41
  53.3 11.1 %collective-permute-start.11 = (bf16[512,256]{1,0:T(8,128)(2,1)S(1)}, bf16[512,256]{1,0:T(8,128)(2,1)S(1)}, u32[]{:S(2)}, u32[]{:S(2)}) collective-permute-start(bf16[512,256]{1,0:T(8,128)(2,1)S(1)} %fusion.14), channel_id=1, source_target_pairs={{0,24},{4,28},{8,16},{12,20},{16,8},{20,12},{24,0},{28,4},{1,25},{... | collective-permute-start | bytes 786440 | tf_op jit(solution)/shard_map/ppermute | solution.py:41
  58.8 6.4 %collective-permute-start.16 = (bf16[512,256]{1,0:T(8,128)(2,1)S(1)}, bf16[512,256]{1,0:T(8,128)(2,1)S(1)}, u32[]{:S(2)}, u32[]{:S(2)}) collective-permute-start(bf16[512,256]{1,0:T(8,128)(2,1)S(1)} %collective-permute-done.9), channel_id=1, source_target_pairs={{0,1},{4,5},{9,10},{13,14},{18,19},{22,23},{27,24},{31,28}} | collective-permute-start | bytes 786440 | tf_op jit(solution)/shard_map/ppermute | solution.py:50
  59.5 6.4 %collective-permute-start.8 = (bf16[256,256]{1,0:T(8,128)(2,1)S(1)}, bf16[256,256]{1,0:T(8,128)(2,1)}, u32[]{:S(2)}, u32[]{:S(2)}) collective-permute-start(bf16[256,256]{1,0:T(8,128)(2,1)S(1)} %constant_dynamic-slice_fusion.4), channel_id=1, source_target_pairs={{0,4},{4,0},{8,12},{12,8},{16,20},{20,16},{24,28},{28,24},{1,5},{5... | collective-permute-start | bytes 393224 | tf_op jit(solution)/shard_map/ppermute | solution.py:38
  59.6 7.3 %collective-permute-start.14 = (bf16[512,256]{1,0:T(8,128)(2,1)S(1)}, bf16[512,256]{1,0:T(8,128)(2,1)S(1)}, u32[]{:S(2)}, u32[]{:S(2)}) collective-permute-start(bf16[512,256]{1,0:T(8,128)(2,1)S(1)} %collective-permute-done.13), channel_id=1, source_target_pairs={{1,2},{5,6},{10,11},{14,15},{19,16},{23,20},{24,25},{28,29}} | collective-permute-start | bytes 786440 | tf_op jit(solution)/shard_map/ppermute | solution.py:50
  63.7 4.5 %collective-permute-start.19 = (bf16[512,256]{1,0:T(8,128)(2,1)S(1)}, bf16[512,256]{1,0:T(8,128)(2,1)S(1)}, u32[]{:S(2)}, u32[]{:S(2)}) collective-permute-start(bf16[512,256]{1,0:T(8,128)(2,1)S(1)} %collective-permute-done.10), channel_id=1, source_target_pairs={{0,1},{4,5},{9,10},{13,14},{18,19},{22,23},{27,24},{31,28}} | collective-permute-start | bytes 786440 | tf_op jit(solution)/shard_map/ppermute | solution.py:50
  64.4 4.5 %collective-permute-start.22 = (bf16[512,256]{1,0:T(8,128)(2,1)S(1)}, bf16[512,256]{1,0:T(8,128)(2,1)S(1)}, u32[]{:S(2)}, u32[]{:S(2)}) collective-permute-start(bf16[512,256]{1,0:T(8,128)(2,1)S(1)} %collective-permute-done.11), channel_id=1, source_target_pairs={{0,1},{4,5},{9,10},{13,14},{18,19},{22,23},{27,24},{31,28}} | collective-permute-start | bytes 786440 | tf_op jit(solution)/shard_map/ppermute | solution.py:50
  65.2 4.5 %collective-permute-start.17 = (bf16[512,256]{1,0:T(8,128)(2,1)S(1)}, bf16[512,256]{1,0:T(8,128)(2,1)S(1)}, u32[]{:S(2)}, u32[]{:S(2)}) collective-permute-start(bf16[512,256]{1,0:T(8,128)(2,1)S(1)} %collective-permute-done.16), channel_id=1, source_target_pairs={{1,2},{5,6},{10,11},{14,15},{19,16},{23,20},{24,25},{28,29}} | collective-permute-start | bytes 786440 | tf_op jit(solution)/shard_map/ppermute | solution.py:50
  66.9 14.4 %collective-permute-start.15 = (bf16[512,256]{1,0:T(8,128)(2,1)S(1)}, bf16[512,256]{1,0:T(8,128)(2,1)S(1)}, u32[]{:S(2)}, u32[]{:S(2)}) collective-permute-start(bf16[512,256]{1,0:T(8,128)(2,1)S(1)} %collective-permute-done.14), channel_id=1, source_target_pairs={{2,3},{6,7},{11,8},{15,12},{16,17},{20,21},{25,26},{29,30}} | collective-permute-start | bytes 786440 | tf_op jit(solution)/shard_map/ppermute | solution.py:50
  68.2 3.6 %collective-permute-start.20 = (bf16[512,256]{1,0:T(8,128)(2,1)S(1)}, bf16[512,256]{1,0:T(8,128)(2,1)S(1)}, u32[]{:S(2)}, u32[]{:S(2)}) collective-permute-start(bf16[512,256]{1,0:T(8,128)(2,1)S(1)} %collective-permute-done.19), channel_id=1, source_target_pairs={{1,2},{5,6},{10,11},{14,15},{19,16},{23,20},{24,25},{28,29}} | collective-permute-start | bytes 786440 | tf_op jit(solution)/shard_map/ppermute | solution.py:50
  68.9 4.2 %collective-permute-start.23 = (bf16[512,256]{1,0:T(8,128)(2,1)S(1)}, bf16[512,256]{1,0:T(8,128)(2,1)S(1)}, u32[]{:S(2)}, u32[]{:S(2)}) collective-permute-start(bf16[512,256]{1,0:T(8,128)(2,1)S(1)} %collective-permute-done.22), channel_id=1, source_target_pairs={{1,2},{5,6},{10,11},{14,15},{19,16},{23,20},{24,25},{28,29}} | collective-permute-start | bytes 786440 | tf_op jit(solution)/shard_map/ppermute | solution.py:50
  69.7 28.5 %collective-permute-start.12 = (bf16[2048,256]{1,0:T(8,128)(2,1)S(1)}, bf16[2048,256]{1,0:T(8,128)(2,1)S(1)}, u32[]{:S(2)}, u32[]{:S(2)}) collective-permute-start(bf16[2048,256]{1,0:T(8,128)(2,1)S(1)} %pad_maximum_fusion.9), channel_id=1, source_target_pairs={{0,4},{4,0},{8,12},{12,8},{16,20},{20,16},{24,28},{28,24},{1,5},{5... | collective-permute-start | bytes 3145736 | tf_op jit(solution)/shard_map/ppermute | solution.py:38
  69.7 18.4 %collective-permute-start.18 = (bf16[512,256]{1,0:T(8,128)(2,1)S(1)}, bf16[512,256]{1,0:T(8,128)(2,1)S(1)}, u32[]{:S(2)}, u32[]{:S(2)}) collective-permute-start(bf16[512,256]{1,0:T(8,128)(2,1)S(1)} %collective-permute-done.17), channel_id=1, source_target_pairs={{2,3},{6,7},{11,8},{15,12},{16,17},{20,21},{25,26},{29,30}} | collective-permute-start | bytes 786440 | tf_op jit(solution)/shard_map/ppermute | solution.py:50
  71.8 21.6 %collective-permute-start.21 = (bf16[512,256]{1,0:T(8,128)(2,1)S(1)}, bf16[512,256]{1,0:T(8,128)(2,1)S(1)}, u32[]{:S(2)}, u32[]{:S(2)}) collective-permute-start(bf16[512,256]{1,0:T(8,128)(2,1)S(1)} %collective-permute-done.20), channel_id=1, source_target_pairs={{2,3},{6,7},{11,8},{15,12},{16,17},{20,21},{25,26},{29,30}} | collective-permute-start | bytes 786440 | tf_op jit(solution)/shard_map/ppermute | solution.py:50
  73.1 25.0 %collective-permute-start.24 = (bf16[512,256]{1,0:T(8,128)(2,1)S(1)}, bf16[512,256]{1,0:T(8,128)(2,1)S(1)}, u32[]{:S(2)}, u32[]{:S(2)}) collective-permute-start(bf16[512,256]{1,0:T(8,128)(2,1)S(1)} %collective-permute-done.23), channel_id=1, source_target_pairs={{2,3},{6,7},{11,8},{15,12},{16,17},{20,21},{25,26},{29,30}} | collective-permute-start | bytes 786440 | tf_op jit(solution)/shard_map/ppermute | solution.py:50
  (8 other events, 44.7 us)

commit v2 on v1

v2 whole, which is shorter than its diff:
```python
import functools
import math

import jax
import jax.numpy as jnp
from jax import lax
from jax.experimental import pallas as pl
from jax.experimental.pallas import tpu as pltpu
from jax.sharding import PartitionSpec as P


length_scale = 0.5
CORES = 2
CHUNKS = 2


def matern(distance):
    scaled = distance * (math.sqrt(3.0) / length_scale)
    return (1.0 + scaled) * jnp.exp(-scaled)


def product(first, second):
    return jnp.dot(first, second, preferred_element_type=jnp.float32)


def transpose_product(first_rows, second_rows):
    return lax.dot_general(
        first_rows, second_rows, (((0,), (0,)), ((), ())), preferred_element_type=jnp.float32
    )


def after(value, *others):
    return lax.optimization_barrier((value, *others))[0]


def in_vmem(value):
    return pltpu.with_memory_space_constraint(value, pltpu.VMEM)


def in_hbm(value):
    return pltpu.with_memory_space_constraint(value, pltpu.HBM)


def keep_wanted(flags, value):
    count = flags.shape[0]
    depth, width = value.shape
    class_of = lax.broadcasted_iota(jnp.int32, (count, width), 0)
    keep = jnp.zeros((count, width), jnp.int32)
    for place in range(count):
        keep = jnp.where(class_of == place, flags[place], keep)
    keep = keep.astype(jnp.float32).astype(value.dtype)
    return (value.reshape(depth // count, count, width) * keep[None]).reshape(depth, width)


def sums_kernel(places, flags, factor, solved, *refs, chips):
    outs = refs[: 2 * CHUNKS]
    masked, solved_in, factor_in, flags_in, sems, solved_sem, flags_sem = refs[2 * CHUNKS :]
    width = outs[0].shape[1]
    half = width * CHUNKS
    block = factor.shape[0] // chips
    flags_copy = pltpu.make_async_copy(flags, flags_in, flags_sem)
    solved_copy = pltpu.make_async_copy(solved, solved_in, solved_sem)
    blocks = [
        pltpu.make_async_copy(
            factor.at[pl.ds(pl.multiple_of((places[0] ^ step) * block, block), block), :],
            factor_in.at[step],
            sems.at[step],
        )
        for step in range(chips)
    ]
    flags_copy.start()
    solved_copy.start()
    blocks[0].start()
    flags_copy.wait()
    solved_copy.wait()
    for copy in blocks[1:]:
        copy.start()

    for core in range(CORES):

        @pl.when(places[1] == core)
        def _():
            for chunk in range(CHUNKS):
                for side, at in ((0, 1 - core), (1, core)):
                    start = at * half + chunk * width
                    column = (chunk * CORES + side) * width
                    masked[:, column : column + width] = keep_wanted(
                        flags_in, solved_in[:, start : start + width]
                    )

    for step in range(chips):
        blocks[step].wait()
        rows = slice(step * block, (step + 1) * block)
        for chunk in range(CHUNKS):
            column = chunk * CORES * width
            sums = jnp.dot(
                factor_in[step],
                masked[:, column : column + CORES * width],
                preferred_element_type=jnp.float32,
            )
            outs[2 * chunk][rows, :] = sums[:, :width].astype(jnp.bfloat16)
            outs[2 * chunk + 1][rows, :] = sums[:, width:]


def partial_sums(places, flags, factor, solved, width, chips):
    rows, depth = factor.shape
    far = pl.BlockSpec(memory_space=pltpu.HBM)
    outs = [
        pltpu.VMEM((rows, width), jnp.bfloat16),
        pltpu.VMEM((rows, width), jnp.float32),
    ] * CHUNKS
    return pl.pallas_call(
        functools.partial(sums_kernel, chips=chips),
        in_specs=[pl.BlockSpec(memory_space=pltpu.SMEM), far, far, far],
        out_specs=[pl.BlockSpec(memory_space=pltpu.VMEM)] * len(outs),
        out_shape=outs,
        scratch_shapes=[
            pltpu.VMEM(solved.shape, solved.dtype),
            pltpu.VMEM(solved.shape, solved.dtype),
            pltpu.VMEM((chips, rows // chips, depth), factor.dtype),
            pltpu.SMEM(flags.shape, flags.dtype),
            pltpu.SemaphoreType.DMA((chips,)),
            pltpu.SemaphoreType.DMA,
            pltpu.SemaphoreType.DMA,
        ],
        compiler_params=pltpu.CompilerParams(vmem_limit_bytes=28 * 2**20),
        name="partial_sums",
    )(places, in_hbm(flags), in_hbm(factor), in_hbm(solved))


def cross_kernel(places, sites, coords, fresh, out):
    count = coords.shape[1]
    rows, columns = out.shape
    chosen = sites[:, pl.ds(pl.multiple_of(places[0] * rows, rows), rows)]
    picked = lax.broadcasted_iota(jnp.int32, (count, rows), 0) == chosen
    picked = jnp.where(picked, 1.0, 0.0).astype(jnp.bfloat16)
    rest = coords[...]
    total = jnp.zeros((coords.shape[0], rows), jnp.float32)
    for _ in range(3):
        part = rest.astype(jnp.bfloat16)
        rest = rest - part.astype(jnp.float32)
        total = total + jnp.dot(part, picked, preferred_element_type=jnp.float32)
    here = jnp.transpose(total)
    start = pl.multiple_of(places[1] * columns, columns)
    there = fresh[:, pl.ds(start, columns)]
    delta_x = here[:, 0:1] - there[0:1, :]
    delta_y = here[:, 1:2] - there[1:2, :]
    out[...] = matern(jnp.sqrt(delta_x * delta_x + delta_y * delta_y))


def cross_tile(places, row_sites, site_coords, new_coords, rows, columns):
    pad = [(0, 8 - site_coords.shape[0]), (0, 0)]
    return pl.pallas_call(
        cross_kernel,
        in_specs=[pl.BlockSpec(memory_space=pltpu.SMEM)]
        + [pl.BlockSpec(memory_space=pltpu.VMEM)] * 3,
        out_specs=pl.BlockSpec(memory_space=pltpu.VMEM),
        out_shape=jax.ShapeDtypeStruct((rows, columns), jnp.float32),
        compiler_params=pltpu.CompilerParams(vmem_limit_bytes=16 * 2**20),
        name="cross_tile",
    )(places, row_sites[None, :], jnp.pad(site_coords, pad), new_coords)


def add_kernel(own, got, *refs):
    outs, (got_in, sem) = refs[:-2], refs[-2:]
    block = outs[0].shape[0]
    copy = pltpu.make_async_copy(got, got_in, sem)
    copy.start()
    copy.wait()
    for at, out in enumerate(outs):
        rows = slice((at + 1) * block, (at + 2) * block)
        out[...] = (own[rows, :] + got_in[rows, :].astype(jnp.float32)).astype(out.dtype)


def add_partner(own, got, chips):
    rows, width = own.shape
    near = pl.BlockSpec(memory_space=pltpu.VMEM)
    return pl.pallas_call(
        add_kernel,
        in_specs=[near, pl.BlockSpec(memory_space=pltpu.HBM)],
        out_specs=[near] * (chips - 1),
        out_shape=[pltpu.VMEM((rows // chips, width), got.dtype)] * (chips - 1),
        scratch_shapes=[pltpu.VMEM((rows, width), got.dtype), pltpu.SemaphoreType.DMA],
        compiler_params=pltpu.CompilerParams(vmem_limit_bytes=16 * 2**20),
        name="add_partner",
    )(in_vmem(own), in_hbm(got))


def make_per_device(row_count, col_count):
    chips = row_count // CORES

    steps = sorted(range(1, chips), key=lambda step: -step.bit_count())
    col_steps = list(range(col_count - 1, 0, -1))

    def to_partner(value):
        return lax.ppermute(value, "row", [(r, r ^ 1) for r in range(row_count)])

    def to_chips(value):
        got = {}
        for step in steps:
            got[step] = lax.ppermute(
                value(step), "row", [(r, r ^ (CORES * step)) for r in range(row_count)]
            )
        return got

    def to_cols(value):
        got = {0: value}
        for step in col_steps:
            got[step] = lax.ppermute(value, "col", [(c, c ^ step) for c in range(col_count)])
        return got

    def per_device(
        panel_index,
        row_sites,
        site_coords,
        new_coords,
        factor_earlier,
        solved_earlier,
        panel_inverse,
        trailing_rhs,
        factor_trailing,
        prior_cov,
    ):
        row_place = lax.axis_index("row")
        col_place = lax.axis_index("col")
        core = row_place % CORES
        chip = row_place // CORES
        local_rows = panel_inverse.shape[0]
        panel_rows = panel_inverse.shape[1]
        earlier_rows = solved_earlier.shape[0]
        new_cols = new_coords.shape[1]
        cov_rows = prior_cov.shape[0]
        class_count = panel_index.shape[0]
        half = new_cols // CORES
        chip_rows = local_rows * CORES

        width = half // CHUNKS
        spans = [slice(q * width, (q + 1) * width) for q in range(CHUNKS)]
        ring = new_cols == CORES * cov_rows and chips == col_count

        if earlier_rows % class_count:
            panel_index = jnp.roll(panel_index, -(row_place * earlier_rows))

        def rows_of(value, step):
            return value[step * chip_rows : (step + 1) * chip_rows]

        places = jnp.stack([chip, core]).astype(jnp.int32)
        sums = partial_sums(
            places, panel_index, factor_earlier, solved_earlier, width, chips
        )
        sent = [to_partner(sums[2 * q]) for q in range(CHUNKS)]
        kept = [sums[2 * q + 1] for q in range(CHUNKS)]
        outgoing = []
        for q in range(CHUNKS):
            if q:
                sent[q] = after(sent[q], outgoing[-1][1])
            added = add_partner(kept[q], sent[q], chips)
            outgoing.append(dict(enumerate(added, start=1)))
        arrived = [to_chips(outgoing[q].get) for q in range(CHUNKS)]

        def relative(value):
            return jnp.concatenate(
                [
                    lax.dynamic_slice_in_dim(value, (chip ^ step) * chip_rows, chip_rows, 1)
                    for step in range(chips)
                ],
                axis=1,
            )

        row_sites, site_coords, new_coords, _ = lax.optimization_barrier(
            (row_sites, site_coords, new_coords, kept[-1])
        )
        cross_cov = cross_tile(places, row_sites, site_coords, new_coords, chip_rows, half)

        inverse_other = to_partner(panel_inverse)
        first_rows = jnp.where(core == 0, panel_inverse, inverse_other)
        second_rows = jnp.where(core == 0, inverse_other, panel_inverse)
        inverse_chip = relative(after(jnp.concatenate([first_rows, second_rows], axis=0), cross_cov))

        right_owns = []
        rights = []
        for q, span in enumerate(spans):
            total = rows_of(kept[q], 0) + rows_of(sent[q], 0)
            for step in steps:
                piece = arrived[q][step]
                if q:
                    piece = after(piece, right_owns[-1])
                total = total + piece.astype(jnp.float32)
            right_own = (cross_cov[:, span] - total).astype(jnp.bfloat16)
            right_owns.append(right_own)
            rights.append(to_chips(lambda step: right_own))

        trailing_factor = relative(after(factor_trailing, *right_owns))

        solved_chunks = []
        mine = []
        columns = []
        for q in range(CHUNKS):
            right = jnp.concatenate(
                [right_owns[q]] + [rights[q][step] for step in range(1, chips)], axis=0
            )
            solved_own = product(inverse_chip, right).astype(jnp.bfloat16)
            solved_chunks.append(solved_own)
            got = to_chips(lambda step: solved_own)
            mine.append(
                jnp.concatenate([solved_own] + [got[step] for step in range(1, chips)], axis=0)
            )
            if ring:
                blocks = to_cols(solved_own)

                def of_chip(step):
                    apart = (chip ^ step) ^ col_place
                    value = blocks[0]
                    for other in col_steps:
                        value = jnp.where(apart == other, blocks[other], value)
                    return value

                spread = to_chips(of_chip)
                columns.append(
                    jnp.concatenate(
                        [of_chip(0)] + [spread[step] for step in range(1, chips)], axis=0
                    )
                )
        theirs = [to_partner(mine[q]) for q in range(CHUNKS)]

        def both(own, others):
            own = jnp.concatenate(own, axis=1)
            others = jnp.concatenate(others, axis=1)
            return jnp.concatenate(
                [jnp.where(core == 0, own, others), jnp.where(core == 0, others, own)], axis=1
            )

        solved_own = jnp.concatenate(solved_chunks, axis=1)
        away = lax.dynamic_slice_in_dim(solved_own, (1 - core) * local_rows, local_rows, 0)
        home = lax.dynamic_slice_in_dim(solved_own, core * local_rows, local_rows, 0)
        solved = both([home], [to_partner(away)])

        gathered = both(mine, theirs)
        trailing_out = trailing_rhs - product(trailing_factor, gathered)
        if ring:
            column_block = jnp.concatenate(columns, axis=1)
        else:
            source = row_place * cov_rows // new_cols
            offset = row_place * cov_rows - source * new_cols
            column_block = lax.dynamic_slice_in_dim(gathered, offset, cov_rows, 1)
            column_block = jnp.where(col_place == source, column_block, jnp.zeros_like(column_block))
            column_block = lax.psum(column_block, "col")
        cond_cov = prior_cov - transpose_product(column_block, gathered) * (1.0 / panel_rows)
        return (solved, trailing_out, cond_cov)

    return per_device


def solution(mesh):
    row_count = mesh.shape["row"]
    col_count = mesh.shape["col"]
    return jax.shard_map(
        make_per_device(row_count, col_count),
        mesh=mesh,
        in_specs=(
            P(),
            P(),
            P(),
            P(None, "col"),
            P(None, "row"),
            P("row", "col"),
            P("row", None),
            P("row", "col"),
            P("row", None),
            P("row", "col"),
        ),
        out_specs=(P("row", "col"), P("row", "col"), P("row", "col")),
        check_vma=False,
    )
```

time: 103 us -> 84.8 us (0.82)
  the two profiles are of different devices: /device:TPU:2 before, /device:TPU:0 now
where the time goes in v2:
time: 84.8 us; the launch traced here: 84.5 us
  starting transfers between devices  42.4 us (50%)
  waiting for transfers between devices  17.8 us (21%)
  Pallas kernels  12.1 us (14%)
  other arithmetic  5.46 us (6%)
  matrix products  4.45 us (5%)
  local copies, waits for them, and re-layouts  1.4 us (2%)
  between operations  0.93 us (1%)
    ppermute x24, starting transfers between devices, to_chips(): lax.ppermute(value(step), 'row', [(r, r ^ CORES * step) for r in range(ro...  30.8 us
    ppermute x6, starting transfers between devices, to_cols(): lax.ppermute(value, 'col', [(c, c ^ step) for c in range(col_count)])  9.87 us
    ppermute x6, waiting for transfers between devices, to_cols(): lax.ppermute(value, 'col', [(c, c ^ step) for c in range(col_count)])  9.73 us
    pallas_call x1, Pallas kernels, partial_sums(): pl.pallas_call(functools.partial(sums_kernel, chips=chips), in_specs=[pl....  7.81 us
    ppermute x24, waiting for transfers between devices, to_chips(): lax.ppermute(value(step), 'row', [(r, r ^ CORES * step) for r in range(ro...  6.23 us
    dot_general x3, matrix products, product(): return jnp.dot(first, second, preferred_element_type=jnp.float32)  2.92 us
    pallas_call x2, Pallas kernels, add_partner(): pl.pallas_call(add_kernel, in_specs=[near, pl.BlockSpec(memory_space=pltp...  2.32 us
    pallas_call x1, Pallas kernels, cross_tile(): pl.pallas_call(cross_kernel, in_specs=[pl.BlockSpec(memory_space=pltpu.SM...  2 us
  transfers between devices with their start and end apart: 36, of which 9 were waited for; matrix products, arithmetic and copies ran while one was open for 11% of the time, Pallas kernels for 5%

profile of v2, /device:TPU:0, one launch (start us, length us, event | category | flops | bytes accessed | tf_op | source)
XLA Modules:
  0.0 84.5 jit_solution(15418813477981272623)
XLA Ops:
  0.7 7.8 %partial_sums.1 = (bf16[2048,128]{1,0:T(8,128)(2,1)S(1)}, f32[2048,128]{1,0:T(8,128)S(1)}, bf16[2048,128]{1,0:T(8,128)(2,1)S(1)}, f32[2048,128]{1,0:T(8,128)S(1)}) custom-call(s32[2]{0:T(128)S(1)} %pad_add_fusion.places, s32[16]{0:T(128)} %flags.1, bf16[2048,2048]{1,0:T(8,128)(2,1)} %factor.1, bf16[2048,512]{1,0:T(8,128)(2,1)} %solved.1), custom_call_target="tpu_custom_call" | custom-call | tf_op jit(solution)/shard_map/partial_sums/pallas_call | solution.py:112
  12.6 2.9 %collective-permute-start.4 = (bf16[512,128]{1,0:T(8,128)(2,1)S(1)}, bf16[512,128]{1,0:T(8,128)(2,1)S(1)}, u32[]{:S(2)}, u32[]{:S(2)}) collective-permute-start(bf16[512,128]{1,0:T(8,128)(2,1)S(1)} %get-tuple-element.31), channel_id=1, source_target_pairs={{0,16},{4,20},{8,24},{12,28},{16,0},{20,4},{24,8},{28,12},{1,17},{... | collective-permute-start | bytes 393224 | tf_op jit(solution)/shard_map/ppermute | solution.py:201
  15.5 1.5 %collective-permute-start.3 = (bf16[512,128]{1,0:T(8,128)(2,1)S(1)}, bf16[512,128]{1,0:T(8,128)(2,1)S(1)}, u32[]{:S(2)}, u32[]{:S(2)}) collective-permute-start(bf16[512,128]{1,0:T(8,128)(2,1)S(1)} %get-tuple-element.30), channel_id=1, source_target_pairs={{0,8},{4,12},{8,0},{12,4},{16,24},{20,28},{24,16},{28,20},{1,9},{5... | collective-permute-start | bytes 393224 | tf_op jit(solution)/shard_map/ppermute | solution.py:201
  17.1 2.0 %cross_tile.1 = f32[512,256]{1,0:T(8,128)S(1)} custom-call(s32[2]{0:T(128)S(1)} %pad_add_fusion.places, s32[1,2048]{1,0:T(1,128)S(1)} %bitcast.3, f32[8,2048]{1,0:T(8,128)S(1)} %pad.4.coords, f32[2,512]{1,0:T(2,128)S(1)} %copy-done.1), custom_call_target="tpu_custom_call" | custom-call | tf_op jit(solution)/shard_map/cross_tile/pallas_call | solution.py:153
  20.3 2.0 %collective-permute-start.11 = (bf16[512,128]{1,0:T(8,128)(2,1)S(1)}, bf16[512,128]{1,0:T(8,128)(2,1)S(1)}, u32[]{:S(2)}, u32[]{:S(2)}) collective-permute-start(bf16[512,128]{1,0:T(8,128)(2,1)S(1)} %get-tuple-element.38), channel_id=1, source_target_pairs={{0,16},{4,20},{8,24},{12,28},{16,0},{20,4},{24,8},{28,12},{1,17},{... | collective-permute-start | bytes 393224 | tf_op jit(solution)/shard_map/ppermute | solution.py:201
  22.4 1.5 %collective-permute-start.10 = (bf16[512,128]{1,0:T(8,128)(2,1)S(1)}, bf16[512,128]{1,0:T(8,128)(2,1)S(1)}, u32[]{:S(2)}, u32[]{:S(2)}) collective-permute-start(bf16[512,128]{1,0:T(8,128)(2,1)S(1)} %get-tuple-element.36), channel_id=1, source_target_pairs={{0,8},{4,12},{8,0},{12,4},{16,24},{20,28},{24,16},{28,20},{1,9},{5... | collective-permute-start | bytes 393224 | tf_op jit(solution)/shard_map/ppermute | solution.py:201
  24.9 2.9 %collective-permute-start.7 = (bf16[512,128]{1,0:T(8,128)(2,1)S(1)}, bf16[512,128]{1,0:T(8,128)(2,1)S(1)}, u32[]{:S(2)}, u32[]{:S(2)}) collective-permute-start(bf16[512,128]{1,0:T(8,128)(2,1)S(1)} %fusion.42), channel_id=1, source_target_pairs={{0,24},{4,28},{8,16},{12,20},{16,8},{20,12},{24,0},{28,4},{1,25},{... | collective-permute-start | bytes 393224 | tf_op jit(solution)/shard_map/ppermute | solution.py:201
  27.9 1.5 %collective-permute-start.6 = (bf16[512,128]{1,0:T(8,128)(2,1)S(1)}, bf16[512,128]{1,0:T(8,128)(2,1)S(1)}, u32[]{:S(2)}, u32[]{:S(2)}) collective-permute-start(bf16[512,128]{1,0:T(8,128)(2,1)S(1)} %fusion.42), channel_id=1, source_target_pairs={{0,16},{4,20},{8,24},{12,28},{16,0},{20,4},{24,8},{28,12},{1,17},{... | collective-permute-start | bytes 393224 | tf_op jit(solution)/shard_map/ppermute | solution.py:201
  29.4 1.8 %collective-permute-done.9 = bf16[512,128]{1,0:T(8,128)(2,1)S(1)} collective-permute-done((bf16[512,128]{1,0:T(8,128)(2,1)S(1)}, bf16[512,128]{1,0:T(8,128)(2,1)S(1)}, u32[]{:S(2)}, u32[]{:S(2)}) %collective-permute-start.9) | collective-permute-done | bytes 131104 | tf_op jit(solution)/shard_map/ppermute | solution.py:201
  32.2 2.3 %collective-permute-start.14 = (bf16[512,128]{1,0:T(8,128)(2,1)S(1)}, bf16[512,128]{1,0:T(8,128)(2,1)S(1)}, u32[]{:S(2)}, u32[]{:S(2)}) collective-permute-start(bf16[512,128]{1,0:T(8,128)(2,1)S(1)} %fusion.41), channel_id=1, source_target_pairs={{0,24},{4,28},{8,16},{12,20},{16,8},{20,12},{24,0},{28,4},{1,25},{... | collective-permute-start | bytes 393224 | tf_op jit(solution)/shard_map/ppermute | solution.py:201
  35.9 1.7 %broadcast_select_fusion.3 = (bf16[256,2048]{1,0:T(8,128)(2,1)S(1)}, bf16[256,2048]{1,0:T(8,128)(2,1)S(1)}) fusion(bf16[256,2048]{1,0:T(8,128)(2,1)} %param.16, bf16[256,2048]{1,0:T(8,128)(2,1)} %collective-permute-done, pred[]{:T(512)S(6)} %eq.28), kind=kLoop, calls=%fused_computation.36 | loop fusion | flops 1048576 | bytes 4194305 | tf_op jit(solution)/shard_map/jit(_where)/select_n | solution.py:276
  41.6 2.1 %collective-permute-start.30 = (bf16[512,128]{1,0:T(8,128)(2,1)S(1)}, bf16[512,128]{1,0:T(8,128)(2,1)S(1)}, u32[]{:S(2)}, u32[]{:S(2)}) collective-permute-start(bf16[512,128]{1,0:T(8,128)(2,1)S(1)} %convolution_convert_fusion), channel_id=1, source_target_pairs={{0,1},{1,0},{2,3},{3,2},{4,5},{5,4},{6,7},{7,6},{8,9},{9,8},{10,11... | collective-permute-start | bytes 393224 | tf_op jit(solution)/shard_map/ppermute | solution.py:209
  43.7 2.6 %collective-permute-start.31 = (bf16[512,128]{1,0:T(8,128)(2,1)S(1)}, bf16[512,128]{1,0:T(8,128)(2,1)S(1)}, u32[]{:S(2)}, u32[]{:S(2)}) collective-permute-start(bf16[512,128]{1,0:T(8,128)(2,1)S(1)} %convolution_convert_fusion), channel_id=1, source_target_pairs={{0,2},{1,3},{2,0},{3,1},{4,6},{5,7},{6,4},{7,5},{8,10},{9,11},{10,... | collective-permute-start | bytes 393224 | tf_op jit(solution)/shard_map/ppermute | solution.py:209
  47.0 2.2 %collective-permute-start.18 = (bf16[512,128]{1,0:T(8,128)(2,1)S(1)}, bf16[512,128]{1,0:T(8,128)(2,1)S(1)}, u32[]{:S(2)}, u32[]{:S(2)}) collective-permute-start(bf16[512,128]{1,0:T(8,128)(2,1)S(1)} %convolution_convert_fusion.1), channel_id=1, source_target_pairs={{0,24},{4,28},{8,16},{12,20},{16,8},{20,12},{24,0},{28,4},{1,25},{... | collective-permute-start | bytes 393224 | tf_op jit(solution)/shard_map/ppermute | solution.py:201
  50.7 5.9 %collective-permute-done.31 = bf16[512,128]{1,0:T(8,128)(2,1)S(1)} collective-permute-done((bf16[512,128]{1,0:T(8,128)(2,1)S(1)}, bf16[512,128]{1,0:T(8,128)(2,1)S(1)}, u32[]{:S(2)}, u32[]{:S(2)}) %collective-permute-start.31) | collective-permute-done | bytes 131104 | tf_op jit(solution)/shard_map/ppermute | solution.py:209
  56.6 1.9 %collective-permute-start.21 = (bf16[512,128]{1,0:T(8,128)(2,1)S(1)}, bf16[512,128]{1,0:T(8,128)(2,1)S(1)}, u32[]{:S(2)}, u32[]{:S(2)}) collective-permute-start(bf16[512,128]{1,0:T(8,128)(2,1)S(1)} %convolution_convert_fusion), channel_id=1, source_target_pairs={{0,24},{4,28},{8,16},{12,20},{16,8},{20,12},{24,0},{28,4},{1,25},{... | collective-permute-start | bytes 393224 | tf_op jit(solution)/shard_map/ppermute | solution.py:201
  61.5 1.7 %collective-permute-start.25 = (bf16[512,128]{1,0:T(8,128)(2,1)S(1)}, bf16[512,128]{1,0:T(8,128)(2,1)S(1)}, u32[]{:S(2)}, u32[]{:S(2)}) collective-permute-start(bf16[512,128]{1,0:T(8,128)(2,1)S(1)} %convolution_convert_fusion.1), channel_id=1, source_target_pairs={{0,2},{1,3},{2,0},{3,1},{4,6},{5,7},{6,4},{7,5},{8,10},{9,11},{10,... | collective-permute-start | bytes 393224 | tf_op jit(solution)/shard_map/ppermute | solution.py:209
  63.2 2.3 %collective-permute-start.26 = (bf16[512,128]{1,0:T(8,128)(2,1)S(1)}, bf16[512,128]{1,0:T(8,128)(2,1)S(1)}, u32[]{:S(2)}, u32[]{:S(2)}) collective-permute-start(bf16[512,128]{1,0:T(8,128)(2,1)S(1)} %convolution_convert_fusion.1), channel_id=1, source_target_pairs={{0,3},{1,2},{2,1},{3,0},{4,7},{5,6},{6,5},{7,4},{8,11},{9,10},{10,... | collective-permute-start | bytes 393224 | tf_op jit(solution)/shard_map/ppermute | solution.py:209
  67.8 1.4 %collective-permute-start.35 = (bf16[512,128]{1,0:T(8,128)(2,1)S(1)}, bf16[512,128]{1,0:T(8,128)(2,1)S(1)}, u32[]{:S(2)}, u32[]{:S(2)}) collective-permute-start(bf16[512,128]{1,0:T(8,128)(2,1)S(1)} %get-tuple-element.58), channel_id=1, source_target_pairs={{0,24},{4,28},{8,16},{12,20},{16,8},{20,12},{24,0},{28,4},{1,25},{... | collective-permute-start | bytes 393224 | tf_op jit(solution)/shard_map/ppermute | solution.py:201
  69.2 3.8 %collective-permute-done.25 = bf16[512,128]{1,0:T(8,128)(2,1)S(1)} collective-permute-done((bf16[512,128]{1,0:T(8,128)(2,1)S(1)}, bf16[512,128]{1,0:T(8,128)(2,1)S(1)}, u32[]{:S(2)}, u32[]{:S(2)}) %collective-permute-start.25) | collective-permute-done | bytes 131104 | tf_op jit(solution)/shard_map/ppermute | solution.py:209
  74.5 2.2 %collective-permute-start.29 = (bf16[512,128]{1,0:T(8,128)(2,1)S(1)}, bf16[512,128]{1,0:T(8,128)(2,1)S(1)}, u32[]{:S(2)}, u32[]{:S(2)}) collective-permute-start(bf16[512,128]{1,0:T(8,128)(2,1)S(1)} %get-tuple-element.54), channel_id=1, source_target_pairs={{0,24},{4,28},{8,16},{12,20},{16,8},{20,12},{24,0},{28,4},{1,25},{... | collective-permute-start | bytes 393224 | tf_op jit(solution)/shard_map/ppermute | solution.py:201
  78.8 1.5 %fusion.2 = f32[256,512]{1,0:T(8,128)} fusion(f32[256,512]{1,0:T(8,128)S(1)} %copy-done.5, bf16[2048,256]{1,0:T(8,128)(2,1)S(1)} %get-tuple-element.42, bf16[2048,256]{1,0:T(8,128)(2,1)S(1)} %get-tuple-element.41, bf16[256,512]{1,0:T(8,128)(2,1)S(1)} %get-tuple-element.50, bf16[256,512]{1,0:T(8,128)(2,1)S(1)} %get-tuple-element.51, ...), kind=kOutput, calls=%fused_computation.5 | convolution fusion | flops 545390592 | bytes 4194304 | tf_op jit(solution)/shard_map/dot_general | solution.py:23
  80.4 1.3 %collective-permute-done.29 = bf16[512,128]{1,0:T(8,128)(2,1)S(1)} collective-permute-done((bf16[512,128]{1,0:T(8,128)(2,1)S(1)}, bf16[512,128]{1,0:T(8,128)(2,1)S(1)}, u32[]{:S(2)}, u32[]{:S(2)}) %collective-permute-start.29) | collective-permute-done | bytes 131104 | tf_op jit(solution)/shard_map/ppermute | solution.py:201
  83.0 1.5 %fusion.4 = f32[256,512]{1,0:T(8,128)} fusion(f32[256,512]{1,0:T(8,128)S(1)} %copy-done.6, bf16[2048,256]{1,0:T(8,128)(2,1)S(1)} %get-tuple-element.42, bf16[2048,256]{1,0:T(8,128)(2,1)S(1)} %get-tuple-element.41, bf16[512,128]{1,0:T(8,128)(2,1)S(1)} %collective-permute-done.35, bf16[512,128]{1,0:T(8,128)(2,1)S(1)} %collective-permute-done.34, ...), kind=kOutput, calls=%fused_computation.7 | convolution fusion | flops 549715968 | bytes 4194304 | tf_op jit(solution)/shard_map/dot_general | solution.py:27
  (88 shorter events, 25.4 us)
Async XLA Ops:
  9.1 10.0 %collective-permute-start.8 = (bf16[2048,128]{1,0:T(8,128)(2,1)S(1)}, bf16[2048,128]{1,0:T(8,128)(2,1)}, u32[]{:S(2)}, u32[]{:S(2)}) collective-permute-start(bf16[2048,128]{1,0:T(8,128)(2,1)S(1)} %get-tuple-element.32), channel_id=1, source_target_pairs={{0,4},{4,0},{8,12},{12,8},{16,20},{20,16},{24,28},{28,24},{1,5},{5... | collective-permute-start | bytes 1572872 | tf_op jit(solution)/shard_map/ppermute | solution.py:196
  9.2 25.9 %collective-permute-start = (bf16[256,2048]{1,0:T(8,128)(2,1)}, bf16[256,2048]{1,0:T(8,128)(2,1)}, u32[]{:S(2)}, u32[]{:S(2)}) collective-permute-start(bf16[256,2048]{1,0:T(8,128)(2,1)} %param.16), channel_id=1, source_target_pairs={{0,4},{4,0},{8,12},{12,8},{16,20},{20,16},{24,28},{28,24},{1,5},{5... | collective-permute-start | bytes 3145736 | tf_op jit(solution)/shard_map/ppermute | solution.py:196
  12.6 9.8 %collective-permute-start.4 = (bf16[512,128]{1,0:T(8,128)(2,1)S(1)}, bf16[512,128]{1,0:T(8,128)(2,1)S(1)}, u32[]{:S(2)}, u32[]{:S(2)}) collective-permute-start(bf16[512,128]{1,0:T(8,128)(2,1)S(1)} %get-tuple-element.31), channel_id=1, source_target_pairs={{0,16},{4,20},{8,24},{12,28},{16,0},{20,4},{24,8},{28,12},{1,17},{... | collective-permute-start | bytes 393224 | tf_op jit(solution)/shard_map/ppermute | solution.py:201
  15.5 8.4 %collective-permute-start.3 = (bf16[512,128]{1,0:T(8,128)(2,1)S(1)}, bf16[512,128]{1,0:T(8,128)(2,1)S(1)}, u32[]{:S(2)}, u32[]{:S(2)}) collective-permute-start(bf16[512,128]{1,0:T(8,128)(2,1)S(1)} %get-tuple-element.30), channel_id=1, source_target_pairs={{0,8},{4,12},{8,0},{12,4},{16,24},{20,28},{24,16},{28,20},{1,9},{5... | collective-permute-start | bytes 393224 | tf_op jit(solution)/shard_map/ppermute | solution.py:201
  20.3 7.5 %collective-permute-start.11 = (bf16[512,128]{1,0:T(8,128)(2,1)S(1)}, bf16[512,128]{1,0:T(8,128)(2,1)S(1)}, u32[]{:S(2)}, u32[]{:S(2)}) collective-permute-start(bf16[512,128]{1,0:T(8,128)(2,1)S(1)} %get-tuple-element.38), channel_id=1, source_target_pairs={{0,16},{4,20},{8,24},{12,28},{16,0},{20,4},{24,8},{28,12},{1,17},{... | collective-permute-start | bytes 393224 | tf_op jit(solution)/shard_map/ppermute | solution.py:201
  22.4 7.0 %collective-permute-start.10 = (bf16[512,128]{1,0:T(8,128)(2,1)S(1)}, bf16[512,128]{1,0:T(8,128)(2,1)S(1)}, u32[]{:S(2)}, u32[]{:S(2)}) collective-permute-start(bf16[512,128]{1,0:T(8,128)(2,1)S(1)} %get-tuple-element.36), channel_id=1, source_target_pairs={{0,8},{4,12},{8,0},{12,4},{16,24},{20,28},{24,16},{28,20},{1,9},{5... | collective-permute-start | bytes 393224 | tf_op jit(solution)/shard_map/ppermute | solution.py:201
  23.9 7.3 %collective-permute-start.9 = (bf16[512,128]{1,0:T(8,128)(2,1)S(1)}, bf16[512,128]{1,0:T(8,128)(2,1)S(1)}, u32[]{:S(2)}, u32[]{:S(2)}) collective-permute-start(bf16[512,128]{1,0:T(8,128)(2,1)S(1)} %get-tuple-element.34), channel_id=1, source_target_pairs={{0,24},{4,28},{8,16},{12,20},{16,8},{20,12},{24,0},{28,4},{1,25},{... | collective-permute-start | bytes 393224 | tf_op jit(solution)/shard_map/ppermute | solution.py:201
  24.9 21.4 %collective-permute-start.7 = (bf16[512,128]{1,0:T(8,128)(2,1)S(1)}, bf16[512,128]{1,0:T(8,128)(2,1)S(1)}, u32[]{:S(2)}, u32[]{:S(2)}) collective-permute-start(bf16[512,128]{1,0:T(8,128)(2,1)S(1)} %fusion.42), channel_id=1, source_target_pairs={{0,24},{4,28},{8,16},{12,20},{16,8},{20,12},{24,0},{28,4},{1,25},{... | collective-permute-start | bytes 393224 | tf_op jit(solution)/shard_map/ppermute | solution.py:201
  27.9 18.4 %collective-permute-start.6 = (bf16[512,128]{1,0:T(8,128)(2,1)S(1)}, bf16[512,128]{1,0:T(8,128)(2,1)S(1)}, u32[]{:S(2)}, u32[]{:S(2)}) collective-permute-start(bf16[512,128]{1,0:T(8,128)(2,1)S(1)} %fusion.42), channel_id=1, source_target_pairs={{0,16},{4,20},{8,24},{12,28},{16,0},{20,4},{24,8},{28,12},{1,17},{... | collective-permute-start | bytes 393224 | tf_op jit(solution)/shard_map/ppermute | solution.py:201
  39.1 7.2 %collective-permute-start.5 = (bf16[512,128]{1,0:T(8,128)(2,1)S(1)}, bf16[512,128]{1,0:T(8,128)(2,1)S(1)}, u32[]{:S(2)}, u32[]{:S(2)}) collective-permute-start(bf16[512,128]{1,0:T(8,128)(2,1)S(1)} %fusion.42), channel_id=1, source_target_pairs={{0,8},{4,12},{8,0},{12,4},{16,24},{20,28},{24,16},{28,20},{1,9},{5... | collective-permute-start | bytes 393224 | tf_op jit(solution)/shard_map/ppermute | solution.py:201
  41.6 8.1 %collective-permute-start.30 = (bf16[512,128]{1,0:T(8,128)(2,1)S(1)}, bf16[512,128]{1,0:T(8,128)(2,1)S(1)}, u32[]{:S(2)}, u32[]{:S(2)}) collective-permute-start(bf16[512,128]{1,0:T(8,128)(2,1)S(1)} %convolution_convert_fusion), channel_id=1, source_target_pairs={{0,1},{1,0},{2,3},{3,2},{4,5},{5,4},{6,7},{7,6},{8,9},{9,8},{10,11... | collective-permute-start | bytes 393224 | tf_op jit(solution)/shard_map/ppermute | solution.py:209
  43.7 12.9 %collective-permute-start.31 = (bf16[512,128]{1,0:T(8,128)(2,1)S(1)}, bf16[512,128]{1,0:T(8,128)(2,1)S(1)}, u32[]{:S(2)}, u32[]{:S(2)}) collective-permute-start(bf16[512,128]{1,0:T(8,128)(2,1)S(1)} %convolution_convert_fusion), channel_id=1, source_target_pairs={{0,2},{1,3},{2,0},{3,1},{4,6},{5,7},{6,4},{7,5},{8,10},{9,11},{10,... | collective-permute-start | bytes 393224 | tf_op jit(solution)/shard_map/ppermute | solution.py:209
  46.3 12.2 %collective-permute-start.32 = (bf16[512,128]{1,0:T(8,128)(2,1)S(1)}, bf16[512,128]{1,0:T(8,128)(2,1)S(1)}, u32[]{:S(2)}, u32[]{:S(2)}) collective-permute-start(bf16[512,128]{1,0:T(8,128)(2,1)S(1)} %convolution_convert_fusion), channel_id=1, source_target_pairs={{0,3},{1,2},{2,1},{3,0},{4,7},{5,6},{6,5},{7,4},{8,11},{9,10},{10,... | collective-permute-start | bytes 393224 | tf_op jit(solution)/shard_map/ppermute | solution.py:209
  47.0 12.0 %collective-permute-start.18 = (bf16[512,128]{1,0:T(8,128)(2,1)S(1)}, bf16[512,128]{1,0:T(8,128)(2,1)S(1)}, u32[]{:S(2)}, u32[]{:S(2)}) collective-permute-start(bf16[512,128]{1,0:T(8,128)(2,1)S(1)} %convolution_convert_fusion.1), channel_id=1, source_target_pairs={{0,24},{4,28},{8,16},{12,20},{16,8},{20,12},{24,0},{28,4},{1,25},{... | collective-permute-start | bytes 393224 | tf_op jit(solution)/shard_map/ppermute | solution.py:201
  49.2 11.0 %collective-permute-start.17 = (bf16[512,128]{1,0:T(8,128)(2,1)S(1)}, bf16[512,128]{1,0:T(8,128)(2,1)S(1)}, u32[]{:S(2)}, u32[]{:S(2)}) collective-permute-start(bf16[512,128]{1,0:T(8,128)(2,1)S(1)} %convolution_convert_fusion.1), channel_id=1, source_target_pairs={{0,16},{4,20},{8,24},{12,28},{16,0},{20,4},{24,8},{28,12},{1,17},{... | collective-permute-start | bytes 393224 | tf_op jit(solution)/shard_map/ppermute | solution.py:201
  49.7 11.7 %collective-permute-start.16 = (bf16[512,128]{1,0:T(8,128)(2,1)S(1)}, bf16[512,128]{1,0:T(8,128)(2,1)S(1)}, u32[]{:S(2)}, u32[]{:S(2)}) collective-permute-start(bf16[512,128]{1,0:T(8,128)(2,1)S(1)} %convolution_convert_fusion.1), channel_id=1, source_target_pairs={{0,8},{4,12},{8,0},{12,4},{16,24},{20,28},{24,16},{28,20},{1,9},{5... | collective-permute-start | bytes 393224 | tf_op jit(solution)/shard_map/ppermute | solution.py:201
  60.2 7.6 %collective-permute-start.24 = (bf16[512,128]{1,0:T(8,128)(2,1)S(1)}, bf16[512,128]{1,0:T(8,128)(2,1)S(1)}, u32[]{:S(2)}, u32[]{:S(2)}) collective-permute-start(bf16[512,128]{1,0:T(8,128)(2,1)S(1)} %convolution_convert_fusion.1), channel_id=1, source_target_pairs={{0,1},{1,0},{2,3},{3,2},{4,5},{5,4},{6,7},{7,6},{8,9},{9,8},{10,11... | collective-permute-start | bytes 393224 | tf_op jit(solution)/shard_map/ppermute | solution.py:209
  61.5 11.5 %collective-permute-start.25 = (bf16[512,128]{1,0:T(8,128)(2,1)S(1)}, bf16[512,128]{1,0:T(8,128)(2,1)S(1)}, u32[]{:S(2)}, u32[]{:S(2)}) collective-permute-start(bf16[512,128]{1,0:T(8,128)(2,1)S(1)} %convolution_convert_fusion.1), channel_id=1, source_target_pairs={{0,2},{1,3},{2,0},{3,1},{4,6},{5,7},{6,4},{7,5},{8,10},{9,11},{10,... | collective-permute-start | bytes 393224 | tf_op jit(solution)/shard_map/ppermute | solution.py:209
  63.2 10.3 %collective-permute-start.26 = (bf16[512,128]{1,0:T(8,128)(2,1)S(1)}, bf16[512,128]{1,0:T(8,128)(2,1)S(1)}, u32[]{:S(2)}, u32[]{:S(2)}) collective-permute-start(bf16[512,128]{1,0:T(8,128)(2,1)S(1)} %convolution_convert_fusion.1), channel_id=1, source_target_pairs={{0,3},{1,2},{2,1},{3,0},{4,7},{5,6},{6,5},{7,4},{8,11},{9,10},{10,... | collective-permute-start | bytes 393224 | tf_op jit(solution)/shard_map/ppermute | solution.py:209
  65.5 9.0 %collective-permute-start.22 = (bf16[2048,128]{1,0:T(8,128)(2,1)S(1)}, bf16[2048,128]{1,0:T(8,128)(2,1)S(1)}, u32[]{:S(2)}, u32[]{:S(2)}) collective-permute-start(bf16[2048,128]{1,0:T(8,128)(2,1)S(1)} %pad_maximum_fusion.11), channel_id=1, source_target_pairs={{0,4},{4,0},{8,12},{12,8},{16,20},{20,16},{24,28},{28,24},{1,5},{5... | collective-permute-start | bytes 1572872 | tf_op jit(solution)/shard_map/ppermute | solution.py:196
  66.8 9.9 %collective-permute-start.23 = (bf16[2048,128]{1,0:T(8,128)(2,1)S(1)}, bf16[2048,128]{1,0:T(8,128)(2,1)S(1)}, u32[]{:S(2)}, u32[]{:S(2)}) collective-permute-start(bf16[2048,128]{1,0:T(8,128)(2,1)S(1)} %pad_maximum_fusion.12), channel_id=1, source_target_pairs={{0,4},{4,0},{8,12},{12,8},{16,20},{20,16},{24,28},{28,24},{1,5},{5... | collective-permute-start | bytes 1572872 | tf_op jit(solution)/shard_map/ppermute | solution.py:196
  67.8 10.0 %collective-permute-start.35 = (bf16[512,128]{1,0:T(8,128)(2,1)S(1)}, bf16[512,128]{1,0:T(8,128)(2,1)S(1)}, u32[]{:S(2)}, u32[]{:S(2)}) collective-permute-start(bf16[512,128]{1,0:T(8,128)(2,1)S(1)} %get-tuple-element.58), channel_id=1, source_target_pairs={{0,24},{4,28},{8,16},{12,20},{16,8},{20,12},{24,0},{28,4},{1,25},{... | collective-permute-start | bytes 393224 | tf_op jit(solution)/shard_map/ppermute | solution.py:201
  73.0 7.4 %collective-permute-start.34 = (bf16[512,128]{1,0:T(8,128)(2,1)S(1)}, bf16[512,128]{1,0:T(8,128)(2,1)S(1)}, u32[]{:S(2)}, u32[]{:S(2)}) collective-permute-start(bf16[512,128]{1,0:T(8,128)(2,1)S(1)} %get-tuple-element.59), channel_id=1, source_target_pairs={{0,16},{4,20},{8,24},{12,28},{16,0},{20,4},{24,8},{28,12},{1,17},{... | collective-permute-start | bytes 393224 | tf_op jit(solution)/shard_map/ppermute | solution.py:201
  74.5 7.2 %collective-permute-start.29 = (bf16[512,128]{1,0:T(8,128)(2,1)S(1)}, bf16[512,128]{1,0:T(8,128)(2,1)S(1)}, u32[]{:S(2)}, u32[]{:S(2)}) collective-permute-start(bf16[512,128]{1,0:T(8,128)(2,1)S(1)} %get-tuple-element.54), channel_id=1, source_target_pairs={{0,24},{4,28},{8,16},{12,20},{16,8},{20,12},{24,0},{28,4},{1,25},{... | collective-permute-start | bytes 393224 | tf_op jit(solution)/shard_map/ppermute | solution.py:201
  (19 other events, 139.2 us)
